TPU v7x, 32 devices: a whole 2x2x4 slice. The times are simulated.
32 devices in a mesh: blk: 8 (over z, y), plane: 4 (over x, core).
Axes of the slice: x: 2, y: 2, z: 4, core: 2. Of those that a mesh axis runs over, the one named last changes fastest.
Arguments:
- tiles: bfloat16 [128, 24, 128, 128], P(('blk', 'plane')), may hold values from -0.25 to 0.25
- tile_cols: int32 [128, 24], P(('blk', 'plane')), may hold values from 0 to 511
- tile_count: int32 [128], P(('blk', 'plane')), may hold values from 18 to 24, as said below
- u_start: float32 [16384], P(('blk', 'plane')), may hold values from -0.046875 to 0.046875
- v_start: float32 [65536], P(('blk', 'plane')), may hold values from -0.0234375 to 0.0234375
- beta_start: float32 [1], replicated, may hold values from 0.5 to 1.5
- left_basis: float32 [16384, 128], P(('blk', 'plane')), may hold values from -0.046875 to 0.046875
- right_basis: float32 [65536, 128], P(('blk', 'plane')), may hold values from -0.0234375 to 0.0234375
Outputs:
- left_vectors: float32 [1, 16384], P(None, ('blk', 'plane'))
- right_vectors: float32 [1, 65536], P(None, ('blk', 'plane'))
- coefficients: float32 [2], replicated
Inputs may be any that keep to these rules, and one draw needn't show every extreme that they name: `tile_count`: slots at and after a row block's count are padding; some row block uses all 24 slots.
All inputs are finite; a program needn't handle non-finite values.
Results may differ from a plain program's by a relative error of at most 0.00055.
The roundings to bfloat16 on the way count: a program that leaves them out, or rounds other values in their place, can miss the bound.
Values may be sent and summed in bfloat16 or wider, within the bound.
No kernel may reach another device: no remote copies, remote signals or barrier semaphores. Data moves between devices by JAX's collectives and lax.ppermute only.
A program may use at most 64 MiB of HBM per device.

v0:
```python
import math
import jax
import jax.numpy as jnp
from jax import lax
from jax.sharding import PartitionSpec as P


def project_twice(vec, basis, gram):
    high = lax.Precision.HIGHEST
    first, whole_sq = lax.psum(
        (jnp.dot(vec, basis, precision=high), jnp.sum(vec * vec)), ("blk", "plane")
    )
    coef = 2.0 * first - jnp.dot(gram, first, precision=high)
    vec = vec - jnp.dot(basis, coef, precision=high)
    total = (
        whole_sq - 2.0 * jnp.sum(coef * first) + jnp.sum(coef * jnp.dot(gram, coef, precision=high))
    )
    norm = jnp.sqrt(total + 1e-06)
    return (vec / norm, norm)


def on_device(tiles, tile_cols, tile_count, u_start, v_start, beta_start, left_basis, right_basis):
    high = lax.Precision.HIGHEST
    devices = lax.axis_size(("blk", "plane"))
    blocks, slots = tile_cols.shape
    n_tiles = v_start.shape[0] * devices // 128
    live = (lax.iota(jnp.int32, slots)[None, :] < tile_count[:, None]).astype(jnp.float32)
    onehot = (tile_cols.reshape(-1)[:, None] == lax.iota(jnp.int32, n_tiles)[None, :]).astype(
        jnp.float32
    )
    left_gram, right_gram = lax.psum(
        (
            jnp.dot(left_basis.T, left_basis, precision=high),
            jnp.dot(right_basis.T, right_basis, precision=high),
        ),
        ("blk", "plane"),
    )
    left_scale = math.sqrt(u_start.shape[0] * devices)
    right_scale = math.sqrt(v_start.shape[0] * devices)
    vec_right = v_start
    vec_left = u_start
    beta = beta_start[0]
    lefts, rights, coefs = ([], [], [])
    rounded = vec_right.astype(jnp.bfloat16)
    whole = lax.all_gather(rounded, ("blk", "plane"), axis=0, tiled=True)
    table = whole.reshape(n_tiles, 128)
    picked = jnp.take(table, tile_cols, axis=0)
    values = jnp.einsum("rsij,rsj->rsi", tiles, picked, preferred_element_type=jnp.float32)
    forward_out = jnp.sum(values * live[:, :, None], axis=1).reshape(-1)
    vec_left, alpha = project_twice(forward_out - beta * vec_left, left_basis, left_gram)
    left_rows = vec_left.astype(jnp.bfloat16).reshape(blocks, 128)
    contrib = jnp.einsum("rsij,ri->rsj", tiles, left_rows, preferred_element_type=jnp.float32)
    contrib = (contrib * live[:, :, None]).reshape(-1, 128)
    partial_value = lax.dot_general(onehot, contrib, (((0,), (0,)), ((), ())), precision=high)
    owned = lax.psum_scatter(partial_value, ("blk", "plane"), scatter_dimension=0, tiled=True)
    back_out = owned.reshape(-1)
    vec_right, beta = project_twice(back_out - alpha * vec_right, right_basis, right_gram)
    lefts.append(vec_left * left_scale)
    rights.append(vec_right * right_scale)
    coefs.append(alpha)
    coefs.append(beta)
    return (jnp.stack(lefts), jnp.stack(rights), jnp.stack(coefs))


def solution(mesh):
    placed = (
        P(("blk", "plane"), None, None, None),
        P(("blk", "plane"), None),
        P(("blk", "plane")),
        P(("blk", "plane")),
        P(("blk", "plane")),
        P(),
        P(("blk", "plane"), None),
        P(("blk", "plane"), None),
    )
    return jax.shard_map(
        on_device,
        mesh=mesh,
        in_specs=placed,
        out_specs=(P(None, ("blk", "plane")), P(None, ("blk", "plane")), P()),
        check_vma=False,
    )
```

profile of v0, /device:TPU:12, one launch (start us, length us, event | category | flops | bytes accessed | tf_op | source)
XLA Modules:
  0.0 338.8 jit_solution(10103056694969738724)
XLA Ops:
  7.2 2.4 fusion.21
  9.6 4.1 %fusion.22 = f32[128,128]{1,0:T(8,128)} fusion(f32[2048,128]{1,0:T(8,128)} %param.15), kind=kOutput, calls=%fused_computation.48 | convolution fusion | flops 402653184 | bytes 1114112 | tf_op jit(solution)/shard_map/dot_general | solution.py:34
  13.8 0.7 compare_and_fusion
  14.5 0.8 eq.15
  15.2 0.7 compare_select_fusion
  16.6 0.7 fusion.12
  17.4 0.7 convert_element_type.14
  18.1 32.0 %all_gather.3 = bf16[65536]{0:T(1024)(128)(2,1)S(1)} all-gather(bf16[2048]{0:T(1024)(128)(2,1)S(1)} %convert_element_type.14), channel_id=1, replica_groups=mesh['blk'=8,'plane'=4] {'blk','plane'}, dimensions={0}, use_global_device_ids=true | all-gather | bytes 135168 | tf_op jit(solution)/shard_map/all_gather | solution.py:45
  50.1 1.3 gather_fusion
  51.4 0.8 select_bitcast_fusion
  52.3 1.7 fusion.8
  54.1 1.3 multiply_reduce_fusion.2
  55.6 49.4 %all-reduce.1 = (f32[128]{0:T(128)S(1)}, f32[]{:T(128)}) all-reduce(f32[128]{0:T(128)S(1)} %convolution_bitcast_fusion.1, f32[]{:T(128)} %get-tuple-element.13), channel_id=1, replica_groups=mesh['blk'=8,'plane'=4] {'blk','plane'}, use_global_device_ids=true, to_apply=%region_1.0 | all-reduce | flops 129 | bytes 1032 | tf_op jit(solution)/shard_map/psum | solution.py:10
  105.0 34.8 %all-reduce.5.cloned.1.call-done = (f32[128,128]{1,0:T(8,128)}, f32[128,128]{1,0:T(8,128)}) async-done(((f32[128,128]{1,0:T(8,128)}, f32[128,128]{1,0:T(8,128)}), (f32[128,128]{1,0:T(8,128)}, f32[128,128]{1,0:T(8,128)})) %all-reduce.5.cloned.1.call-update) | async-done | bytes 131088 | tf_op jit(solution)/shard_map/psum | solution.py:31
  139.8 1.7 multiply_reduce_fusion.4
  141.5 1.7 fusion.4
  146.1 1.2 fusion.6
  147.9 106.2 %reduce-scatter.2.cloned.1.call-done = f32[16,128]{1,0:T(8,128)} async-done(((f32[512,128]{1,0:T(8,128)}), f32[16,128]{1,0:T(8,128)}) %reduce-scatter.2.cloned.1.call-update) | async-done | bytes 8208 | tf_op jit(solution)/shard_map/reduce_scatter | solution.py:55
  254.1 1.3 multiply_reduce_fusion.1
  255.4 1.8 convolution_bitcast_fusion
  257.2 67.5 %all-reduce = (f32[128]{0:T(128)S(1)}, f32[]{:T(128)}) all-reduce(f32[128]{0:T(128)S(1)} %convolution_bitcast_fusion, f32[]{:T(128)} %get-tuple-element.9), channel_id=1, replica_groups=mesh['blk'=8,'plane'=4] {'blk','plane'}, use_global_device_ids=true, to_apply=%region_8.9 | all-reduce | flops 129 | bytes 1032 | tf_op jit(solution)/shard_map/psum | solution.py:10
  324.8 0.8 multiply_reduce_fusion.3
  325.6 0.9 fusion.5
  326.5 2.2 fusion.14
  (23 shorter events, 3.2 us)
Async XLA Ops:
  7.2 45.1 %copy-start = (bf16[4,24,128,128]{3,2,1,0:T(8,128)(2,1)S(1)}, bf16[4,24,128,128]{3,2,1,0:T(8,128)(2,1)}, u32[]{:S(2)}) copy-start(bf16[4,24,128,128]{3,2,1,0:T(8,128)(2,1)} %param.8) | copy-start | bytes 9437188
  7.2 132.6 %all-reduce.5.cloned.1.call-start = ((), (), s32[]{:S(2)}) async-start(), calls=%async_computation.2 | async-start | bytes 262144 | tf_op jit(solution)/shard_map/psum | solution.py:31
  9.6 45.8 %copy-start.1 = (f32[512,128]{1,0:T(8,128)S(1)}, f32[512,128]{1,0:T(8,128)}, u32[]{:S(2)}) copy-start(f32[512,128]{1,0:T(8,128)} %param.14) | copy-start | bytes 786436
  13.7 240.3 %reduce-scatter.2.cloned.1.call-start = ((), (), s32[]{:S(2)}) async-start(), calls=%async_computation.1 | async-start | bytes 270336 | tf_op jit(solution)/shard_map/reduce_scatter | solution.py:55
  52.2 201.9 %copy-start.3 = (f32[2048]{0:T(1024)S(1)}, f32[2048]{0:T(1024)}, u32[]{:S(2)}) copy-start(f32[2048]{0:T(1024)} %param.12) | copy-start | bytes 24580
  139.8 185.0 %copy-start.2 = (f32[128,128]{1,0:T(8,128)S(1)}, f32[128,128]{1,0:T(8,128)}, u32[]{:S(2)}) copy-start(f32[128,128]{1,0:T(8,128)} %get-tuple-element.8) | copy-start | bytes 196612
Sparse Core Ops, SparseCore 0:
  13.9 125.9 all-reduce.4
  147.4 106.6 reduce-scatter.1
where the time goes:
time: 340 us; the launch traced here: 339 us
  blocking collectives  149 us (44%)
  waiting for transfers between devices  141 us (41%)
  matrix products  19.5 us (6%)
  between operations  18.8 us (6%)
  other arithmetic  8.19 us (2%)
    psum x2, blocking collectives, project_twice(): lax.psum((jnp.dot(vec, basis, precision=high), jnp.sum(vec * vec)), ('blk...  117 us
    reduce_scatter x1, waiting for transfers between devices, on_device(): lax.psum_scatter(partial_value, ('blk', 'plane'), scatter_dimension=0, ti...  106 us
    psum x1, waiting for transfers between devices, on_device(): lax.psum((jnp.dot(left_basis.T, left_basis, precision=high), jnp.dot(righ...  34.8 us
    all_gather x1, blocking collectives, on_device(): whole = lax.all_gather(rounded, ('blk', 'plane'), axis=0, tiled=True)  32 us
  transfers between devices with their start and end apart: 2, of which 2 were waited for; matrix products, arithmetic and copies ran while one was open for 3% of the time, Pallas kernels for 0%

commit v1 on v0

--- a/solution.py
+++ b/solution.py
@@ -8,7 +8,7 @@
 def project_twice(vec, basis, gram):
     high = lax.Precision.HIGHEST
     first, whole_sq = lax.psum(
-        (jnp.dot(vec, basis, precision=high), jnp.sum(vec * vec)), ("blk", "plane")
+        lax.psum((jnp.dot(vec, basis, precision=high), jnp.sum(vec * vec)), "plane"), "blk"
     )
     coef = 2.0 * first - jnp.dot(gram, first, precision=high)
     vec = vec - jnp.dot(basis, coef, precision=high)

time: 340 us -> 326 us (0.959); the launches traced: 339 us -> 321 us
  blocking collectives: 149 us -> 114 us
  waiting for transfers between devices: 141 us -> 158 us
    psum x2 -> x4, blocking collectives: 117 us -> 82.2 us  [the longest x2 69.2 us: project_twice(): lax.psum(lax.psum((jnp.dot(vec, basis, precision=high), jnp.sum(vec * vec...]
    psum x1, waiting for transfers between devices: 34.8 us -> 52.1 us  [on_device(): lax.psum((jnp.dot(left_basis.T, left_basis, precision=high), jnp.dot(righ...]
where the time goes in v1:
time: 326 us; the launch traced here: 321 us
  waiting for transfers between devices  158 us (48%)
  blocking collectives  114 us (35%)
  matrix products  19.5 us (6%)
  between operations  18.8 us (6%)
  other arithmetic  8.19 us (3%)
    reduce_scatter x1, waiting for transfers between devices, on_device(): lax.psum_scatter(partial_value, ('blk', 'plane'), scatter_dimension=0, ti...  106 us
    psum x2, blocking collectives, project_twice(): lax.psum(lax.psum((jnp.dot(vec, basis, precision=high), jnp.sum(vec * vec...  69.2 us
    psum x1, waiting for transfers between devices, on_device(): lax.psum((jnp.dot(left_basis.T, left_basis, precision=high), jnp.dot(righ...  52.1 us
    all_gather x1, blocking collectives, on_device(): whole = lax.all_gather(rounded, ('blk', 'plane'), axis=0, tiled=True)  32 us
    psum x2, blocking collectives, project_twice(): lax.psum((jnp.dot(vec, basis, precision=high), jnp.sum(vec * vec)), 'plane')  13 us
  transfers between devices with their start and end apart: 2, of which 2 were waited for; matrix products, arithmetic and copies ran while one was open for 3% of the time, Pallas kernels for 0%

profile of v1, /device:TPU:12, one launch (start us, length us, event | category | flops | bytes accessed | tf_op | source)
XLA Modules:
  0.0 321.2 jit_solution(8883117752325938917)
XLA Ops:
  7.2 2.4 fusion.21
  9.6 4.1 %fusion.22 = f32[128,128]{1,0:T(8,128)} fusion(f32[2048,128]{1,0:T(8,128)} %param.15), kind=kOutput, calls=%fused_computation.48 | convolution fusion | flops 402653184 | bytes 1114112 | tf_op jit(solution)/shard_map/dot_general | solution.py:34
  14.5 0.8 eq.15
  16.6 0.7 fusion.12
  17.4 0.7 convert_element_type.14
  18.1 32.0 %all_gather.3 = bf16[65536]{0:T(1024)(128)(2,1)S(1)} all-gather(bf16[2048]{0:T(1024)(128)(2,1)S(1)} %convert_element_type.14), channel_id=1, replica_groups=mesh['blk'=8,'plane'=4] {'blk','plane'}, dimensions={0}, use_global_device_ids=true | all-gather | bytes 135168 | tf_op jit(solution)/shard_map/all_gather | solution.py:45
  50.1 1.3 gather_fusion
  51.4 0.8 select_bitcast_fusion
  52.3 1.7 fusion.8
  54.1 1.3 multiply_reduce_fusion.2
  55.6 6.6 %all-reduce.4 = (f32[128]{0:T(128)S(1)}, f32[]{:T(128)}) all-reduce(f32[128]{0:T(128)S(1)} %convolution_bitcast_fusion.1, f32[]{:T(128)} %get-tuple-element.17), channel_id=1, replica_groups=mesh['blk'=8,'plane'=4] {'plane'}, use_global_device_ids=true, to_apply=%region_1.0 | all-reduce | flops 129 | bytes 1032 | tf_op jit(solution)/shard_map/psum | solution.py:11
  62.2 25.5 %all-reduce.2 = (f32[128]{0:T(128)S(1)}, f32[]{:T(128)}) all-reduce(f32[128]{0:T(128)S(1)} %get-tuple-element.11, f32[]{:T(128)} %get-tuple-element.12), channel_id=1, replica_groups=mesh['blk'=8,'plane'=4] {'blk'}, use_global_device_ids=true, to_apply=%region_2.3 | all-reduce | flops 129 | bytes 1032 | tf_op jit(solution)/shard_map/psum | solution.py:10
  87.7 52.1 %all-reduce.7.cloned.1.call-done = (f32[128,128]{1,0:T(8,128)}, f32[128,128]{1,0:T(8,128)}) async-done(((f32[128,128]{1,0:T(8,128)}, f32[128,128]{1,0:T(8,128)}), (f32[128,128]{1,0:T(8,128)}, f32[128,128]{1,0:T(8,128)})) %all-reduce.7.cloned.1.call-update) | async-done | bytes 131088 | tf_op jit(solution)/shard_map/psum | solution.py:31
  139.8 1.7 multiply_reduce_fusion.4
  141.5 1.7 fusion.4
  146.1 1.2 fusion.6
  147.9 106.2 %reduce-scatter.2.cloned.1.call-done = f32[16,128]{1,0:T(8,128)} async-done(((f32[512,128]{1,0:T(8,128)}), f32[16,128]{1,0:T(8,128)}) %reduce-scatter.2.cloned.1.call-update) | async-done | bytes 8208 | tf_op jit(solution)/shard_map/reduce_scatter | solution.py:55
  254.1 1.3 multiply_reduce_fusion.1
  255.4 1.8 convolution_bitcast_fusion
  257.2 6.4 %all-reduce.3 = (f32[128]{0:T(128)S(1)}, f32[]{:T(128)}) all-reduce(f32[128]{0:T(128)S(1)} %convolution_bitcast_fusion, f32[]{:T(128)} %get-tuple-element.13), channel_id=1, replica_groups=mesh['blk'=8,'plane'=4] {'plane'}, use_global_device_ids=true, to_apply=%region_10.11 | all-reduce | flops 129 | bytes 1032 | tf_op jit(solution)/shard_map/psum | solution.py:11
  263.6 43.7 %all-reduce.1 = (f32[128]{0:T(128)S(1)}, f32[]{:T(128)}) all-reduce(f32[128]{0:T(128)S(1)} %get-tuple-element.9, f32[]{:T(128)} %get-tuple-element.10), channel_id=1, replica_groups=mesh['blk'=8,'plane'=4] {'blk'}, use_global_device_ids=true, to_apply=%region_11.12 | all-reduce | flops 129 | bytes 1032 | tf_op jit(solution)/shard_map/psum | solution.py:10
  307.3 0.8 multiply_reduce_fusion.3
  308.1 0.9 fusion.5
  309.0 2.2 fusion.14
  (25 shorter events, 4.6 us)
Async XLA Ops:
  7.2 45.1 %copy-start = (bf16[4,24,128,128]{3,2,1,0:T(8,128)(2,1)S(1)}, bf16[4,24,128,128]{3,2,1,0:T(8,128)(2,1)}, u32[]{:S(2)}) copy-start(bf16[4,24,128,128]{3,2,1,0:T(8,128)(2,1)} %param.8) | copy-start | bytes 9437188
  7.2 132.6 %all-reduce.7.cloned.1.call-start = ((), (), s32[]{:S(2)}) async-start(), calls=%async_computation.2 | async-start | bytes 262144 | tf_op jit(solution)/shard_map/psum | solution.py:31
  9.6 45.8 %copy-start.1 = (f32[512,128]{1,0:T(8,128)S(1)}, f32[512,128]{1,0:T(8,128)}, u32[]{:S(2)}) copy-start(f32[512,128]{1,0:T(8,128)} %param.14) | copy-start | bytes 786436
  13.7 240.3 %reduce-scatter.2.cloned.1.call-start = ((), (), s32[]{:S(2)}) async-start(), calls=%async_computation.1 | async-start | bytes 270336 | tf_op jit(solution)/shard_map/reduce_scatter | solution.py:55
  52.2 201.8 %copy-start.3 = (f32[2048]{0:T(1024)S(1)}, f32[2048]{0:T(1024)}, u32[]{:S(2)}) copy-start(f32[2048]{0:T(1024)} %param.12) | copy-start | bytes 24580
  139.8 167.5 %copy-start.2 = (f32[128,128]{1,0:T(8,128)S(1)}, f32[128,128]{1,0:T(8,128)}, u32[]{:S(2)}) copy-start(f32[128,128]{1,0:T(8,128)} %get-tuple-element.4) | copy-start | bytes 196612
Sparse Core Ops, SparseCore 0:
  13.9 125.8 all-reduce.6
  147.4 106.6 reduce-scatter.1

commit v2 on v0

--- a/solution.py
+++ b/solution.py
@@ -29,11 +29,14 @@
         jnp.float32
     )
     left_gram, right_gram = lax.psum(
-        (
-            jnp.dot(left_basis.T, left_basis, precision=high),
-            jnp.dot(right_basis.T, right_basis, precision=high),
+        lax.psum(
+            (
+                jnp.dot(left_basis.T, left_basis, precision=high),
+                jnp.dot(right_basis.T, right_basis, precision=high),
+            ),
+            "blk",
         ),
-        ("blk", "plane"),
+        "plane",
     )
     left_scale = math.sqrt(u_start.shape[0] * devices)
     right_scale = math.sqrt(v_start.shape[0] * devices)

time: 340 us -> 326 us (0.959)
  blocking collectives: 149 us -> 140 us
  waiting for transfers between devices: 141 us -> 136 us
    psum x2, blocking collectives: 117 us -> 108 us  [project_twice(): lax.psum((jnp.dot(vec, basis, precision=high), jnp.sum(vec * vec)), ('blk...]
    psum x1, waiting for transfers between devices: 34.8 us -> 29.1 us  [on_device(): lax.psum((jnp.dot(left_basis.T, left_basis, precision=high), jnp.dot(righ...]
  transfers between devices with their start and end apart: 2 -> 3, of which waited for: 2 -> 2; matrix products, arithmetic and copies ran while one was open for 3% -> 3% of each run, Pallas kernels for 0% -> 0%
where the time goes in v2:
time: 326 us; the launch traced here: 325 us
  blocking collectives  140 us (43%)
  waiting for transfers between devices  136 us (42%)
  matrix products  19.4 us (6%)
  between operations  18.5 us (6%)
  other arithmetic  8.7 us (3%)
    psum x2, blocking collectives, project_twice(): lax.psum((jnp.dot(vec, basis, precision=high), jnp.sum(vec * vec)), ('blk...  108 us
    reduce_scatter x1, waiting for transfers between devices, on_device(): lax.psum_scatter(partial_value, ('blk', 'plane'), scatter_dimension=0, ti...  107 us
    all_gather x1, blocking collectives, on_device(): whole = lax.all_gather(rounded, ('blk', 'plane'), axis=0, tiled=True)  32 us
    psum x1, waiting for transfers between devices, on_device(): lax.psum((jnp.dot(left_basis.T, left_basis, precision=high), jnp.dot(righ...  29.1 us
  transfers between devices with their start and end apart: 3, of which 2 were waited for; matrix products, arithmetic and copies ran while one was open for 3% of the time, Pallas kernels for 0%

profile of v2, /device:TPU:12, one launch (start us, length us, event | category | flops | bytes accessed | tf_op | source)
XLA Modules:
  0.0 325.0 jit_solution(6327846638119417009)
XLA Ops:
  7.2 2.4 fusion.21
  9.6 4.0 %fusion.22 = f32[128,128]{1,0:T(8,128)} fusion(f32[2048,128]{1,0:T(8,128)} %param.15), kind=kOutput, calls=%fused_computation.48 | convolution fusion | flops 402653184 | bytes 1114112 | tf_op jit(solution)/shard_map/dot_general | solution.py:35
  13.7 1.2 compare_and_fusion
  14.9 0.8 eq.15
  15.7 0.7 compare_select_fusion
  17.0 0.7 fusion.12
  17.8 0.7 convert_element_type.14
  18.5 32.0 %all_gather.3 = bf16[65536]{0:T(1024)(128)(2,1)S(1)} all-gather(bf16[2048]{0:T(1024)(128)(2,1)S(1)} %convert_element_type.14), channel_id=1, replica_groups=mesh['blk'=8,'plane'=4] {'blk','plane'}, dimensions={0}, use_global_device_ids=true | all-gather | bytes 135168 | tf_op jit(solution)/shard_map/all_gather | solution.py:48
  50.6 1.3 gather_fusion
  51.8 0.8 select_bitcast_fusion
  52.7 1.7 fusion.8
  54.5 1.3 multiply_reduce_fusion.2
  55.8 29.1 %all-reduce.7.cloned.1.call-done = (f32[128,128]{1,0:T(8,128)}, f32[128,128]{1,0:T(8,128)}) async-done(((f32[128,128]{1,0:T(8,128)}, f32[128,128]{1,0:T(8,128)}), (f32[128,128]{1,0:T(8,128)}, f32[128,128]{1,0:T(8,128)})) %all-reduce.7.cloned.1.call-update) | async-done | bytes 131088 | tf_op jit(solution)/shard_map/psum | solution.py:32
  85.2 40.3 %all-reduce.1 = (f32[128]{0:T(128)S(1)}, f32[]{:T(128)}) all-reduce(f32[128]{0:T(128)S(1)} %convolution_bitcast_fusion.1, f32[]{:T(128)} %get-tuple-element.15), channel_id=1, replica_groups=mesh['blk'=8,'plane'=4] {'blk','plane'}, use_global_device_ids=true, to_apply=%region_1.0 | all-reduce | flops 129 | bytes 1032 | tf_op jit(solution)/shard_map/psum | solution.py:10
  125.6 1.7 multiply_reduce_fusion.4
  127.3 1.7 fusion.4
  131.8 1.2 fusion.6
  133.6 107.0 %reduce-scatter.2.cloned.1.call-done = f32[16,128]{1,0:T(8,128)} async-done(((f32[512,128]{1,0:T(8,128)}), f32[16,128]{1,0:T(8,128)}) %reduce-scatter.2.cloned.1.call-update) | async-done | bytes 8208 | tf_op jit(solution)/shard_map/reduce_scatter | solution.py:58
  240.6 1.3 multiply_reduce_fusion.1
  241.9 1.8 convolution_bitcast_fusion
  243.7 67.6 %all-reduce = (f32[128]{0:T(128)S(1)}, f32[]{:T(128)}) all-reduce(f32[128]{0:T(128)S(1)} %convolution_bitcast_fusion, f32[]{:T(128)} %get-tuple-element.11), channel_id=1, replica_groups=mesh['blk'=8,'plane'=4] {'blk','plane'}, use_global_device_ids=true, to_apply=%region_9.10 | all-reduce | flops 129 | bytes 1032 | tf_op jit(solution)/shard_map/psum | solution.py:10
  311.3 0.8 multiply_reduce_fusion.3
  312.1 0.9 fusion.5
  313.0 2.2 fusion.14
  (26 shorter events, 3.3 us)
Async XLA Ops:
  7.2 45.5 %copy-start = (bf16[4,24,128,128]{3,2,1,0:T(8,128)(2,1)S(1)}, bf16[4,24,128,128]{3,2,1,0:T(8,128)(2,1)}, u32[]{:S(2)}) copy-start(bf16[4,24,128,128]{3,2,1,0:T(8,128)(2,1)} %param.8) | copy-start | bytes 9437188
  7.2 77.8 %all-reduce.7.cloned.1.call-start = ((), (), s32[]{:S(2)}) async-start(), calls=%async_computation.2 | async-start | bytes 262144 | tf_op jit(solution)/shard_map/psum | solution.py:32
  9.6 75.4 %copy-start.1 = (f32[512,128]{1,0:T(8,128)S(1)}, f32[512,128]{1,0:T(8,128)}, u32[]{:S(2)}) copy-start(f32[512,128]{1,0:T(8,128)} %param.14) | copy-start | bytes 786436
  13.7 111.9 %all-reduce.9.cloned.1.call-start = ((), (), s32[]{:S(2)}) async-start(), calls=%async_computation.3 | async-start | bytes 262144 | tf_op jit(solution)/shard_map/psum | solution.py:31
  54.4 186.2 %copy-start.3 = (f32[2048]{0:T(1024)S(1)}, f32[2048]{0:T(1024)}, u32[]{:S(2)}) copy-start(f32[2048]{0:T(1024)} %param.12) | copy-start | bytes 24580
  85.0 155.6 %reduce-scatter.2.cloned.1.call-start = ((), (), s32[]{:S(2)}) async-start(), calls=%async_computation.1 | async-start | bytes 270336 | tf_op jit(solution)/shard_map/reduce_scatter | solution.py:58
  125.6 185.7 %copy-start.2 = (f32[128,128]{1,0:T(8,128)S(1)}, f32[128,128]{1,0:T(8,128)}, u32[]{:S(2)}) copy-start(f32[128,128]{1,0:T(8,128)} %get-tuple-element.10) | copy-start | bytes 196612
Sparse Core Ops, SparseCore 0:
  13.8 71.1 all-reduce.6
  87.3 31.5 all-reduce.8
  133.2 107.3 reduce-scatter.1
